TPU v7x, 32 devices: a whole 2x2x4 slice. The times are simulated.
32 devices in a mesh: dp: 2 (over x), fsdp: 16 (over z, y, core).
Axes of the slice: x: 2, y: 2, z: 4, core: 2. Of those that a mesh axis runs over, the one named last changes fastest.
Arguments:
- tokens: bfloat16 [18432, 768], P(('dp', 'fsdp')), may hold values from -6 to 6
- gain_attn: bfloat16 [768], P(('dp', 'fsdp')), may hold values from 0.25 to 1.75
- w_qkv: bfloat16 [768, 2304], P(('dp', 'fsdp')), may hold values from -0.21875 to 0.21875
- w_proj: bfloat16 [768, 768], P(('dp', 'fsdp')), may hold values from -2.5 to 2.5
- gain_moe: bfloat16 [768], P(('dp', 'fsdp')), may hold values from 0.25 to 1.75
- w_router: bfloat16 [768, 8], P(('dp', 'fsdp')), may hold values from -0.15625 to 0.15625
- w_in: bfloat16 [8, 768, 3072], P('dp', 'fsdp'), may hold values from -0.21875 to 0.21875
- w_out: bfloat16 [8, 3072, 768], P('dp', 'fsdp'), may hold values from -0.875 to 0.875
- routes: int32 [18432, 2], P(('dp', 'fsdp')), may hold values from 0 to 7, as said below
- slot_ids: int32 [18432, 2], P(('dp', 'fsdp')), may hold values from 0 to 152, as said below
- cotangent: bfloat16 [18432, 768], P(('dp', 'fsdp')), may hold values from -6 to 6
Outputs:
- output: bfloat16 [18432, 768], P(('dp', 'fsdp'))
- grad_tokens: float32 [18432, 768], P(('dp', 'fsdp'))
- d_gain_attn: float32 [768], P(('dp', 'fsdp'))
- d_qkv: float32 [768, 2304], P(('dp', 'fsdp'))
- d_proj: float32 [768, 768], P(('dp', 'fsdp'))
- d_gain_moe: float32 [768], P(('dp', 'fsdp'))
- d_router: float32 [768, 8], P(('dp', 'fsdp'))
- d_in: float32 [8, 768, 3072], P('dp', 'fsdp')
- d_out: float32 [8, 3072, 768], P('dp', 'fsdp')
Inputs may be any that keep to these rules, and one draw needn't show every extreme that they name: `routes`: each row names two different experts. `slot_ids`: among the 576 patches of one device, the pairs routed to one expert hold the distinct slots 0, 1, 2, ... in some priority order; a pair beyond the 152 slots holds 152 and is dropped. On every device some expert gets more than 152 pairs.
All inputs are finite; a program needn't handle non-finite values.
Results may differ from a plain program's by a relative error of at most 0.017.
Values may be sent and summed in bfloat16 or wider, within the bound.
No kernel may reach another device: no remote copies, remote signals or barrier semaphores. Data moves between devices by JAX's collectives and lax.ppermute only.
A program may use at most 320 MiB of HBM per device.

v0:
```python
import jax
import jax.numpy as jnp
from jax import lax
from jax.sharding import PartitionSpec as P

HEADS = 12
HEAD_DIM = 64
EXPERTS = 8
SEQ = 576
CAP = 152
norm_epsilon = 1e-06


def norm_parts(values):
    centre = values - jnp.mean(values, axis=-1, keepdims=True)
    inverse = lax.rsqrt(jnp.mean(centre * centre, axis=-1, keepdims=True) + norm_epsilon)
    return (centre * inverse, inverse)


def norm_back(grad_normed, normed, inverse):
    mean_grad = jnp.mean(grad_normed, axis=-1, keepdims=True)
    mean_cross = jnp.mean(grad_normed * normed, axis=-1, keepdims=True)
    return (grad_normed - mean_grad - normed * mean_cross) * inverse


def gelu_tanh(values):
    return jax.nn.gelu(values, approximate=True)


def head_forward(operands):
    queries, keys_head, values_head = operands
    scores = jnp.einsum(
        "isd,itd->ist", queries, keys_head, preferred_element_type=jnp.float32
    ) * HEAD_DIM ** (-0.5)
    largest = jnp.max(scores, axis=-1, keepdims=True)
    powers = jnp.exp(scores - largest)
    totals = jnp.sum(powers, axis=-1, keepdims=True)
    attn_probs = (powers / totals).astype(jnp.bfloat16)
    head_out = jnp.einsum(
        "ist,itd->isd", attn_probs, values_head, preferred_element_type=jnp.float32
    )
    return (head_out.astype(jnp.bfloat16), (largest + jnp.log(totals))[..., 0])


def head_backward(operands):
    queries, keys_head, values_head, grad_head, log_total = operands
    scores = jnp.einsum(
        "isd,itd->ist", queries, keys_head, preferred_element_type=jnp.float32
    ) * HEAD_DIM ** (-0.5)
    attn_probs = jnp.exp(scores - log_total[..., None])
    grad_probs = jnp.einsum(
        "isd,itd->ist", grad_head, values_head, preferred_element_type=jnp.float32
    )
    row_terms = jnp.sum(attn_probs * grad_probs, axis=-1, keepdims=True)
    grad_scores = (attn_probs * (grad_probs - row_terms)).astype(jnp.bfloat16)
    grad_query = jnp.einsum(
        "ist,itd->isd", grad_scores, keys_head, preferred_element_type=jnp.float32
    ) * HEAD_DIM ** (-0.5)
    grad_key = jnp.einsum(
        "ist,isd->itd", grad_scores, queries, preferred_element_type=jnp.float32
    ) * HEAD_DIM ** (-0.5)
    grad_value = jnp.einsum(
        "ist,isd->itd",
        attn_probs.astype(jnp.bfloat16),
        grad_head,
        preferred_element_type=jnp.float32,
    )
    return (grad_query, grad_key, grad_value)


def expert_forward(expert_rows, w_up, w_down):
    pre_act = jnp.einsum("ecd,edf->ecf", expert_rows, w_up, preferred_element_type=jnp.float32)
    hidden = gelu_tanh(pre_act).astype(jnp.bfloat16)
    result = jnp.einsum("ecf,efd->ecd", hidden, w_down, preferred_element_type=jnp.float32).astype(
        jnp.bfloat16
    )
    return (pre_act, hidden, result)


def expert_backward(expert_rows, pre_act, hidden, grad_result, w_up, w_down):
    grad_hidden = jnp.einsum(
        "ecd,efd->ecf", grad_result, w_down, preferred_element_type=jnp.float32
    )
    ignored, pull_back = jax.vjp(gelu_tanh, pre_act)
    grad_pre = pull_back(grad_hidden)[0].astype(jnp.bfloat16)
    grad_down = jnp.einsum("ecf,ecd->efd", hidden, grad_result, preferred_element_type=jnp.float32)
    grad_up = jnp.einsum("ecd,ecf->edf", expert_rows, grad_pre, preferred_element_type=jnp.float32)
    grad_rows = jnp.einsum(
        "ecf,edf->ecd", grad_pre, w_up, preferred_element_type=jnp.float32
    ).astype(jnp.bfloat16)
    return (grad_up, grad_down, grad_rows)


def gather_dense(gain_attn, w_qkv, w_proj, gain_moe, w_router):
    return (
        lax.all_gather(gain_attn, ("dp", "fsdp"), axis=0, tiled=True),
        lax.all_gather(w_qkv, ("dp", "fsdp"), axis=0, tiled=True),
        lax.all_gather(w_proj, ("dp", "fsdp"), axis=0, tiled=True),
        lax.all_gather(gain_moe, ("dp", "fsdp"), axis=0, tiled=True),
        lax.all_gather(w_router, ("dp", "fsdp"), axis=0, tiled=True),
    )


def gather_experts(w_in, w_out):
    local_pair = (w_in, w_out)
    return (
        lax.all_gather(local_pair[0], "fsdp", axis=1, tiled=True),
        lax.all_gather(local_pair[1], "fsdp", axis=1, tiled=True),
    )


def reduce_experts(grad_up, grad_down):
    reduced = (
        lax.psum_scatter(
            grad_up.astype(jnp.bfloat16), "fsdp", scatter_dimension=1, tiled=True
        ).astype(jnp.float32),
        lax.psum_scatter(
            grad_down.astype(jnp.bfloat16), "fsdp", scatter_dimension=1, tiled=True
        ).astype(jnp.float32),
    )
    return reduced


def per_device(
    tokens, gain_attn, w_qkv, w_proj, gain_moe, w_router, w_in, w_out, routes, slot_ids, cotangent
):
    dense_full = gather_dense(gain_attn, w_qkv, w_proj, gain_moe, w_router)
    expert_weights = gather_experts(w_in, w_out)
    rows_here = tokens.shape[0]
    images = rows_here // SEQ
    residual = tokens.astype(jnp.float32)
    normed_one, inverse_one = norm_parts(residual)
    gain_one = dense_full[0].astype(jnp.float32)
    act_one = (normed_one * gain_one).astype(jnp.bfloat16)
    qkv = jnp.dot(act_one, dense_full[1], preferred_element_type=jnp.float32).astype(jnp.bfloat16)
    split_qkv = qkv.reshape(images, SEQ, 3, HEADS, HEAD_DIM).transpose(2, 3, 0, 1, 4)
    head_out, head_lse = lax.map(head_forward, (split_qkv[0], split_qkv[1], split_qkv[2]))
    attended = head_out.transpose(1, 2, 0, 3).reshape(rows_here, -1)
    resid_mid = residual + jnp.dot(attended, dense_full[2], preferred_element_type=jnp.float32)
    normed_two, inverse_two = norm_parts(resid_mid)
    gain_two = dense_full[3].astype(jnp.float32)
    act_two = (normed_two * gain_two).astype(jnp.bfloat16)
    logits = jnp.dot(act_two, dense_full[4], preferred_element_type=jnp.float32)
    router = jax.nn.softmax(logits, axis=-1)
    expert_ids = lax.broadcasted_iota(jnp.int32, (1, 1, EXPERTS), 2)
    chosen = routes[:, :, None] == expert_ids
    gate_values = jnp.sum(jnp.where(chosen, router[:, None, :], 0.0), axis=-1)
    gates_low = gate_values.astype(jnp.bfloat16)
    slot_count = EXPERTS * CAP
    columns = lax.broadcasted_iota(jnp.int32, (1, 1, slot_count), 2)
    live_pair = slot_ids < CAP
    targets = routes * CAP + slot_ids
    matches = (targets[:, :, None] == columns) & live_pair[:, :, None]
    dispatch = jnp.sum(matches.astype(jnp.bfloat16), axis=1)
    combine = jnp.sum(
        jnp.where(matches, gates_low[:, :, None], jnp.zeros((), jnp.bfloat16)), axis=1
    )
    slot_rows = (
        jnp.einsum("tx,td->xd", dispatch, act_two, preferred_element_type=jnp.float32)
        .astype(jnp.bfloat16)
        .reshape(EXPERTS, CAP, -1)
    )
    expert_rows = lax.all_to_all(slot_rows, "dp", split_axis=0, concat_axis=1, tiled=True)
    pre_act, hidden, result = expert_forward(expert_rows, expert_weights[0], expert_weights[1])
    slot_result = lax.all_to_all(result, "dp", split_axis=1, concat_axis=0, tiled=True)
    flat_result = slot_result.reshape(slot_count, -1)
    moe_sum = jnp.einsum("tx,xd->td", combine, flat_result, preferred_element_type=jnp.float32)
    output = (resid_mid + moe_sum).astype(jnp.bfloat16)
    dense_full = gather_dense(gain_attn, w_qkv, w_proj, gain_moe, w_router)
    expert_weights = gather_experts(w_in, w_out)
    grad_slots = (
        jnp.einsum("tx,td->xd", combine, cotangent, preferred_element_type=jnp.float32)
        .astype(jnp.bfloat16)
        .reshape(EXPERTS, CAP, -1)
    )
    picked = flat_result[jnp.clip(targets, 0, slot_count - 1)]
    grad_gates = jnp.where(
        live_pair,
        jnp.einsum("tkd,td->tk", picked, cotangent, preferred_element_type=jnp.float32),
        0.0,
    )
    grad_router = jnp.sum(jnp.where(chosen, grad_gates[:, :, None], 0.0), axis=1)
    grad_logits = (
        router * (grad_router - jnp.sum(router * grad_router, axis=-1, keepdims=True))
    ).astype(jnp.bfloat16)
    d_router = jnp.einsum("td,te->de", act_two, grad_logits, preferred_element_type=jnp.float32)
    grad_act_two = jnp.einsum(
        "te,de->td", grad_logits, dense_full[4], preferred_element_type=jnp.float32
    )
    grad_expert = lax.all_to_all(grad_slots, "dp", split_axis=0, concat_axis=1, tiled=True)
    grad_up, grad_down, grad_rows = expert_backward(
        expert_rows, pre_act, hidden, grad_expert, expert_weights[0], expert_weights[1]
    )
    grad_rows = lax.all_to_all(grad_rows, "dp", split_axis=1, concat_axis=0, tiled=True)
    grad_act_two = grad_act_two + jnp.einsum(
        "tx,xd->td", dispatch, grad_rows.reshape(slot_count, -1), preferred_element_type=jnp.float32
    )
    d_gain_moe = jnp.sum(grad_act_two * normed_two, axis=0)
    grad_mid = cotangent.astype(jnp.float32) + norm_back(
        grad_act_two * gain_two, normed_two, inverse_two
    )
    grad_mid_low = grad_mid.astype(jnp.bfloat16)
    d_proj = jnp.einsum("td,te->de", attended, grad_mid_low, preferred_element_type=jnp.float32)
    grad_attended = jnp.einsum(
        "te,de->td", grad_mid_low, dense_full[2], preferred_element_type=jnp.float32
    ).astype(jnp.bfloat16)
    grad_heads = grad_attended.reshape(images, SEQ, HEADS, HEAD_DIM).transpose(2, 0, 1, 3)
    grad_query, grad_key, grad_value = lax.map(
        head_backward, (split_qkv[0], split_qkv[1], split_qkv[2], grad_heads, head_lse)
    )
    grad_qkv = (
        jnp.stack([grad_query, grad_key, grad_value])
        .transpose(2, 3, 0, 1, 4)
        .reshape(rows_here, -1)
        .astype(jnp.bfloat16)
    )
    d_qkv = jnp.einsum("td,te->de", act_one, grad_qkv, preferred_element_type=jnp.float32)
    grad_act_one = jnp.einsum(
        "te,de->td", grad_qkv, dense_full[1], preferred_element_type=jnp.float32
    )
    d_gain_attn = jnp.sum(grad_act_one * normed_one, axis=0)
    grad_tokens = grad_mid + norm_back(grad_act_one * gain_one, normed_one, inverse_one)
    dense_grads = (
        lax.psum_scatter(d_gain_attn, ("dp", "fsdp"), scatter_dimension=0, tiled=True),
        lax.psum_scatter(d_qkv, ("dp", "fsdp"), scatter_dimension=0, tiled=True),
        lax.psum_scatter(d_proj, ("dp", "fsdp"), scatter_dimension=0, tiled=True),
        lax.psum_scatter(d_gain_moe, ("dp", "fsdp"), scatter_dimension=0, tiled=True),
        lax.psum_scatter(d_router, ("dp", "fsdp"), scatter_dimension=0, tiled=True),
    )
    expert_grads = reduce_experts(grad_up, grad_down)
    return (
        output,
        grad_tokens,
        dense_grads[0],
        dense_grads[1],
        dense_grads[2],
        dense_grads[3],
        dense_grads[4],
        expert_grads[0],
        expert_grads[1],
    )


def solution(mesh):
    in_specs = (
        P(("dp", "fsdp"), None),
        P(("dp", "fsdp")),
        P(("dp", "fsdp"), None),
        P(("dp", "fsdp"), None),
        P(("dp", "fsdp")),
        P(("dp", "fsdp"), None),
        P("dp", "fsdp", None),
        P("dp", "fsdp", None),
        P(("dp", "fsdp"), None),
        P(("dp", "fsdp"), None),
        P(("dp", "fsdp"), None),
    )
    out_specs = (
        P(("dp", "fsdp"), None),
        P(("dp", "fsdp"), None),
        P(("dp", "fsdp")),
        P(("dp", "fsdp"), None),
        P(("dp", "fsdp"), None),
        P(("dp", "fsdp")),
        P(("dp", "fsdp"), None),
        P("dp", "fsdp", None),
        P("dp", "fsdp", None),
    )
    return jax.shard_map(
        per_device, mesh=mesh, in_specs=in_specs, out_specs=out_specs, check_vma=False
    )
```

profile of v0, /device:TPU:0, one launch (start us, length us, event | category | flops | bytes accessed | tf_op | source)
XLA Modules:
  0.0 1001.7 jit_solution(7998535637937780949)
XLA Ops:
  10.6 42.0 %all-reduce.6 = (bf16[768]{0:T(1024)(128)(2,1)S(1)}, bf16[768]{0:T(1024)(128)(2,1)S(1)}) all-reduce(bf16[768]{0:T(1024)(128)(2,1)S(1)} %dynamic-update-slice, bf16[768]{0:T(1024)(128)(2,1)S(1)} %dynamic-update-slice.1), channel_id=1, replica_groups=mesh['dp'=2,'fsdp'=16] {'dp','fsdp'}, use_global_device_ids=true, to_apply=%add | all-reduce | flops 1536 | bytes 6144
  52.6 40.8 %all-gather = bf16[32,24,8]{1,2,0:T(8,128)(2,1)S(1)} all-gather(bf16[1,24,8]{1,2,0:T(8,128)(2,1)S(1)} %bitcast.199), channel_id=1, replica_groups=mesh['dp'=2,'fsdp'=16] {'dp','fsdp'}, dimensions={0}, use_global_device_ids=true | all-gather | bytes 12672 | tf_op jit(solution)/shard_map/all_gather | solution.py:100
  95.4 5.9 convolution_convert_fusion.3
  101.3 4.0 copy.102
  113.4 37.9 %while.26 = (s32[]{:T(128)}, bf16[12,1,576,64]{2,3,1,0:T(8,128)(2,1)}, f32[12,1,576]{2,1,0:T(1,128)}, bf16[12,1,576,64]{3,2,1,0:T(8,128)(2,1)S(1)}, bf16[12,1,57...) while((s32[]{:T(128)}, bf16[12,1,576,64]{2,3,1,0:T(8,128)(2,1)}, ...), condition=%wide.region_5.6_spmd, body=%wide.region_2.5_spmd.sunk | while | flops 87293376 | bytes 4531033 | solution.py:137
  151.3 4.1 fusion.75
  167.5 4.4 convolution_convert_fusion.5
  171.9 18.5 %all-to-all-done.2 = bf16[8,152,768]{2,1,0:T(8,128)(2,1)S(1)} async-done(((bf16[8,152,768]{2,1,0:T(8,128)(2,1)}), bf16[8,152,768]{2,1,0:T(8,128)(2,1)S(1)}, u32[]{:S(2)}, u32[]{:S(2)}) %all-to-all-start.2) | async-done | bytes 1867808 | tf_op jit(solution)/shard_map/all_to_all | solution.py:190
  191.7 4.8 all-to-all-start
  198.6 20.2 %all-to-all-done = bf16[8,152,768]{2,1,0:T(8,128)(2,1)} async-done(((bf16[8,152,768]{2,1,0:T(8,128)(2,1)}), bf16[8,152,768]{2,1,0:T(8,128)(2,1)}, u32[]{:S(2)}, u32[]{:S(2)}) %all-to-all-start) | async-done | bytes 1867808 | tf_op jit(solution)/shard_map/all_to_all | solution.py:163
  221.7 7.1 all-gather.12.cloned.1.call-done
  228.8 12.9 %fusion.77 = f32[4,304,3072]{2,1,0:T(8,128)} fusion(bf16[4,304,768]{2,1,0:T(8,128)(2,1)S(1)} %bitcast.182, bf16[4,3072,768]{2,1,0:T(8,128)(2,1)} %all-gather.12.cloned.1.call-done), kind=kOutput, calls=%fused_computation.141 | convolution fusion | flops 5737807872 | bytes 35684352 | tf_op jit(solution)/shard_map/ecd,efd->ecf/dot_general | solution.py:81
  241.7 87.4 %all-gather.10.cloned.1.call-done = bf16[4,768,3072]{2,1,0:T(8,128)(2,1)} async-done(((bf16[4,48,3072]{2,1,0:T(8,128)(2,1)}), bf16[4,768,3072]{2,1,0:T(8,128)(2,1)}) %all-gather.10.cloned.1.call-update) | async-done | bytes 18874384 | tf_op jit(solution)/shard_map/all_gather | solution.py:107
  329.1 26.9 %fusion.43 = (bf16[4,304,3072]{2,1,0:T(8,128)(2,1)}, f32[4,304,3072]{2,1,0:T(8,128)}) fusion(f32[4,304,3072]{2,1,0:T(8,128)} %fusion.77, bf16[4,304,768]{2,1,0:T(8,128)(2,1)} %bitcast.192, bf16[4,768,3072]{2,1,0:T(8,128)(2,1)} %all-gather.10.cloned.1.call-done), kind=kOutput, calls=%fused_computation.59 | convolution fusion | flops 5812518912 | bytes 58097664 | tf_op jit(solution)/shard_map/ecd,edf->ecf/dot_general | solution.py:72
  356.0 16.5 %convolution_convert_fusion.2 = bf16[4,768,3072]{2,1,0:T(8,128)(2,1)} fusion(bf16[4,304,768]{2,1,0:T(8,128)(2,1)} %bitcast.193, bf16[4,304,3072]{2,1,0:T(8,128)(2,1)} %get-tuple-element.212), kind=kOutput, calls=%fused_computation.62 | convolution fusion | flops 5747245056 | bytes 28213248 | tf_op jit(solution)/shard_map/ecd,ecf->edf/dot_general | solution.py:87
  372.8 20.0 %convolution_convert_fusion.1 = bf16[4,3072,768]{2,1,0:T(8,128)(2,1)} fusion(bf16[4,304,768]{2,1,0:T(8,128)(2,1)S(1)} %bitcast.183, f32[4,304,3072]{2,1,0:T(8,128)} %get-tuple-element.213), kind=kOutput, calls=%fused_computation.61 | convolution fusion | flops 5780865024 | bytes 35684352 | tf_op jit(solution)/shard_map/ecf,ecd->efd/dot_general | solution.py:86
  392.9 19.3 %convolution_convert_fusion.7 = bf16[4,304,768]{2,1,0:T(8,128)(2,1)S(1)} fusion(bf16[4,3072,768]{2,1,0:T(8,128)(2,1)} %all-gather.12.cloned.1.call-done, f32[4,304,3072]{2,1,0:T(8,128)} %get-tuple-element.213), kind=kOutput, calls=%fused_computation.85 | convolution fusion | flops 5772361728 | bytes 35684352 | tf_op jit(solution)/shard_map/ecf,efd->ecd/dot_general | solution.py:74
  418.4 13.2 %convolution_convert_fusion.6 = bf16[4,304,768]{2,1,0:T(8,128)(2,1)} fusion(bf16[4,304,3072]{2,1,0:T(8,128)(2,1)} %get-tuple-element.212, bf16[4,768,3072]{2,1,0:T(8,128)(2,1)} %all-gather.10.cloned.1.call-done), kind=kOutput, calls=%fused_computation.84 | convolution fusion | flops 5738741760 | bytes 28213248 | tf_op jit(solution)/shard_map/ecf,edf->ecd/dot_general | solution.py:88
  435.3 6.1 all-to-all-done.1
  442.6 4.8 all-to-all-start.3
  449.7 20.1 %all-to-all-done.3 = bf16[4,304,768]{2,0,1:T(4,128)(2,1)} async-done(((bf16[4,304,768]{2,0,1:T(4,128)(2,1)}), bf16[4,304,768]{2,0,1:T(4,128)(2,1)}, u32[]{:S(2)}, u32[]{:S(2)}) %all-to-all-start.3) | async-done | bytes 1867808 | tf_op jit(solution)/shard_map/all_to_all | solution.py:194
  472.9 4.8 gather_fusion
  477.7 4.7 reshape.217
  482.4 6.0 fusion.62
  499.1 4.3 fusion.66
  503.7 100.7 %while.27 = (s32[]{:T(128)}, bf16[12,1,576,64]{2,3,1,0:T(8,128)(2,1)}, bf16[12,1,576,64]{2,3,1,0:T(8,128)(2,1)}, bf16[12,1,576,64]{2,3,1,0:T(8,128)(2,1)}, bf16[...) while((s32[]{:T(128)}, ...), condition=%wide.region_19.20_spmd, body=%wide.region_17.19_spmd.sunk | while | flops 215064000 | bytes 11510129 | solution.py:208
  608.4 5.5 fusion.71
  615.2 7.2 fusion.60
  622.4 43.2 %all-reduce.5 = (f32[768]{0:T(1024)S(1)}, f32[768]{0:T(1024)S(1)}, f32[768,8]{0,1:T(8,128)S(1)}) all-reduce(f32[768]{0:T(1024)S(1)} %get-tuple-element.158, f32[768]{0:T(1024)S(1)} %get-tuple-element.156, f32[768,8]{0,1:T(8,128)S(1)} %fusion.79), channel_id=2, replica_groups=mesh['dp'=2,'fsdp'=16] {'dp','fsdp'}, use_global_device_ids=true, to_apply=%region_23.24.clone | all-reduce | flops 7680 | bytes 61440
  676.7 88.2 %reduce-scatter.12.cloned.1.call-done = bf16[4,192,768]{2,1,0:T(8,128)(2,1)} async-done(((bf16[4,3072,768]{2,1,0:T(8,128)(2,1)}), bf16[4,192,768]{2,1,0:T(8,128)(2,1)}) %reduce-scatter.12.cloned.1.call-update) | async-done | bytes 1179664 | tf_op jit(solution)/shard_map/reduce_scatter | solution.py:117
  767.8 101.8 %reduce-scatter.8.cloned.1.call-done = f32[24,768]{1,0:T(8,128)} async-done(((f32[768,768]{1,0:T(8,128)}), f32[24,768]{1,0:T(8,128)}) %reduce-scatter.8.cloned.1.call-update) | async-done | bytes 73744 | tf_op jit(solution)/shard_map/reduce_scatter | solution.py:226
  869.6 124.8 %reduce-scatter.6.cloned.1.call-done = f32[24,2304]{1,0:T(8,128)} async-done(((f32[768,2304]{1,0:T(8,128)}), f32[24,2304]{1,0:T(8,128)}) %reduce-scatter.6.cloned.1.call-update) | async-done | bytes 221200 | tf_op jit(solution)/shard_map/reduce_scatter | solution.py:225
  (308 shorter events, 216.5 us)
Async XLA Ops:
  7.2 2.9 copy-start.36
  7.2 3.1 copy-start.37
  7.2 45.4 %copy-start.34 = (bf16[24,8]{0,1:T(8,128)(2,1)S(1)}, bf16[24,8]{0,1:T(8,128)(2,1)}, u32[]{:S(2)}) copy-start(bf16[24,8]{0,1:T(8,128)(2,1)} %param.20) | copy-start | bytes 1156
  7.2 86.3 %copy-start.8 = (bf16[576,768]{1,0:T(8,128)(2,1)S(1)}, bf16[576,768]{1,0:T(8,128)(2,1)}, u32[]{:S(2)}) copy-start(bf16[576,768]{1,0:T(8,128)(2,1)} %param.15) | copy-start | bytes 2654212
  7.2 88.2 %all-gather.6.cloned.1.call-start = ((), (), s32[]{:S(2)}) async-start(), calls=%async_computation.8 | async-start | bytes 3649536 | tf_op jit(solution)/shard_map/all_gather | solution.py:97
  8.0 143.4 %all-gather.8.cloned.1.call-start = ((), (), s32[]{:S(2)}) async-start(), calls=%async_computation.9 | async-start | bytes 1216512 | tf_op jit(solution)/shard_map/all_gather | solution.py:98
  8.7 220.1 %all-gather.12.cloned.1.call-start = ((), (), s32[]{:S(2)}) async-start(), calls=%async_computation.11 | async-start | bytes 20054016 | tf_op jit(solution)/shard_map/all_gather | solution.py:108
  9.4 84.7 %copy-start.21 = (s32[576,2]{0,1:T(2,128)S(1)}, s32[576,2]{0,1:T(2,128)}, u32[]{:S(2)}) copy-start(s32[576,2]{0,1:T(2,128)} %param.24) | copy-start | bytes 13828
  9.4 85.3 %copy-start.23 = (s32[576,2]{0,1:T(2,128)S(1)}, s32[576,2]{0,1:T(2,128)}, u32[]{:S(2)}) copy-start(s32[576,2]{0,1:T(2,128)} %param.23) | copy-start | bytes 13828
  9.5 319.6 %all-gather.10.cloned.1.call-start = ((), (), s32[]{:S(2)}) async-start(), calls=%async_computation.10 | async-start | bytes 20054016 | tf_op jit(solution)/shard_map/all_gather | solution.py:107
  52.6 42.8 %copy-start.29 = (f32[768]{0:T(1024)}, f32[768]{0:T(1024)S(1)}, u32[]{:S(2)}) copy-start(f32[768]{0:T(1024)S(1)} %convert_element_type.101) | copy-start | bytes 9220
  151.3 4.1 copy-start.4
  151.3 4.2 copy-start.5
  156.7 10.9 %copy-start.6 = (bf16[576,768]{1,0:T(8,128)(2,1)}, bf16[576,768]{1,0:T(8,128)(2,1)S(1)}, u32[]{:S(2)}) copy-start(bf16[576,768]{1,0:T(8,128)(2,1)S(1)} %multiply_convert_fusion.2) | copy-start | bytes 2654212
  156.7 4.2 copy-start.19
  160.9 2.9 copy-start.14
  163.8 26.7 %all-to-all-start.2 = ((bf16[8,152,768]{2,1,0:T(8,128)(2,1)}), bf16[8,152,768]{2,1,0:T(8,128)(2,1)S(1)}, u32[]{:S(2)}, u32[]{:S(2)}) async-start(bf16[8,152,768]{2,1,0:T(8,128)(2,1)} %bitcast.194), calls=%async_computation.2 | async-start | bytes 3735552 | tf_op jit(solution)/shard_map/all_to_all | solution.py:190
  191.7 27.1 %all-to-all-start = ((bf16[8,152,768]{2,1,0:T(8,128)(2,1)}), bf16[8,152,768]{2,1,0:T(8,128)(2,1)}, u32[]{:S(2)}, u32[]{:S(2)}) async-start(bf16[8,152,768]{2,1,0:T(8,128)(2,1)} %bitcast.191), calls=%async_computation | async-start | bytes 3735552 | tf_op jit(solution)/shard_map/all_to_all | solution.py:163
  196.5 477.2 %reduce-scatter.10.cloned.1.call-start = ((), (), s32[]{:S(2)}) async-start(), calls=%async_computation.14 | async-start | bytes 20054016 | tf_op jit(solution)/shard_map/reduce_scatter | solution.py:114
  372.6 392.4 %reduce-scatter.12.cloned.1.call-start = ((), (), s32[]{:S(2)}) async-start(), calls=%async_computation.15 | async-start | bytes 20054016 | tf_op jit(solution)/shard_map/reduce_scatter | solution.py:117
  414.4 27.0 %all-to-all-start.1 = ((bf16[4,304,768]{2,0,1:T(4,128)(2,1)}), bf16[4,304,768]{2,0,1:T(4,128)(2,1)S(1)}, u32[]{:S(2)}, u32[]{:S(2)}) async-start(bf16[4,304,768]{2,0,1:T(4,128)(2,1)} %copy.108), calls=%async_computation.1 | async-start | bytes 3735552 | tf_op jit(solution)/shard_map/all_to_all | solution.py:165
  435.3 12.2 %copy-start.28 = (s32[576,2]{0,1:T(2,128)S(1)}, s32[576,2]{0,1:T(2,128)}, u32[]{:S(2)}) copy-start(s32[576,2]{0,1:T(2,128)} %get-tuple-element.199) | copy-start | bytes 13828
  442.6 27.1 %all-to-all-start.3 = ((bf16[4,304,768]{2,0,1:T(4,128)(2,1)}), bf16[4,304,768]{2,0,1:T(4,128)(2,1)}, u32[]{:S(2)}, u32[]{:S(2)}) async-start(bf16[4,304,768]{2,0,1:T(4,128)(2,1)} %copy.112), calls=%async_computation.3 | async-start | bytes 3735552 | tf_op jit(solution)/shard_map/all_to_all | solution.py:194
  447.4 422.2 %reduce-scatter.8.cloned.1.call-start = ((), (), s32[]{:S(2)}) async-start(), calls=%async_computation.13 | async-start | bytes 2433024 | tf_op jit(solution)/shard_map/reduce_scatter | solution.py:226
  482.4 7.1 copy-start.22
  482.4 7.3 copy-start.16
  489.7 3.0 copy-start.1
  503.4 491.0 %reduce-scatter.6.cloned.1.call-start = ((), (), s32[]{:S(2)}) async-start(), calls=%async_computation.12 | async-start | bytes 7299072 | tf_op jit(solution)/shard_map/reduce_scatter | solution.py:225
  606.2 2.2 copy-start.32
  615.2 52.2 %copy-start.10 = (bf16[576,768]{1,0:T(8,128)(2,1)S(1)}, bf16[576,768]{1,0:T(8,128)(2,1)}, u32[]{:S(2)}) copy-start(bf16[576,768]{1,0:T(8,128)(2,1)} %param.15) | copy-start | bytes 2654212
  667.4 4.0 copy-start.2
  667.4 4.0 copy-start.15
  (18 other events, 26.8 us)
Sparse Core Ops, SparseCore 0:
  10.9 62.6 all-gather.5
  76.6 52.6 all-gather.7
  130.9 97.8 all-gather.11
  230.2 98.8 all-gather.9
  372.7 194.0 reduce-scatter.9
  570.7 194.1 reduce-scatter.11
  770.8 98.7 reduce-scatter.7
  875.8 118.5 reduce-scatter.5
where the time goes:
time: 1010 us; the launch traced here: 1000 us
  waiting for transfers between devices  477 us (47%)
  matrix products  276 us (27%)
  blocking collectives  126 us (12%)
  local copies, waits for them, and re-layouts  66.9 us (7%)
  other arithmetic  22.4 us (2%)
  starting transfers between devices  18.3 us (2%)
  between operations  15.1 us (1%)
    reduce_scatter x1, waiting for transfers between devices, per_device(): lax.psum_scatter(d_qkv, ('dp', 'fsdp'), scatter_dimension=0, tiled=True)  125 us
    reduce_scatter x1, waiting for transfers between devices, per_device(): lax.psum_scatter(d_proj, ('dp', 'fsdp'), scatter_dimension=0, tiled=True)  102 us
    reduce_scatter x1, waiting for transfers between devices, reduce_experts(): lax.psum_scatter(grad_down.astype(jnp.bfloat16), 'fsdp', scatter_dimensio...  88.2 us
    all_gather x1, waiting for transfers between devices, gather_experts(): lax.all_gather(local_pair[0], 'fsdp', axis=1, tiled=True)  87.4 us
    unnamed x2, blocking collectives  85.2 us
    all_gather x1, blocking collectives, gather_dense(): lax.all_gather(w_router, ('dp', 'fsdp'), axis=0, tiled=True)  40.8 us
    dot_general x1, matrix products, expert_forward(): jnp.einsum('ecd,edf->ecf', expert_rows, w_up, preferred_element_type=jnp....  26.9 us
    dot_general x12, matrix products, head_forward(): jnp.einsum('ist,itd->isd', attn_probs, values_head, preferred_element_typ...  23.4 us
  transfers between devices with their start and end apart: 12, of which 9 were waited for; matrix products, arithmetic and copies ran while one was open for 31% of the time, Pallas kernels for 0%

commit v1 on v0

--- a/solution.py
+++ b/solution.py
@@ -103,8 +103,38 @@
 
 def gather_experts(w_in, w_out):
     local_pair = (w_in, w_out)
+
+    def process_terms(on_dim, peer_axis, message):
+        view_out = lax.axis_size(peer_axis)
+        f_next = lax.axis_index(peer_axis)
+        formed, q_next, current_value = (view_out, f_next, message.shape[on_dim])
+        t_next = tuple(
+            (
+                hop_no * formed if dev == on_dim else hop_no
+                for dev, hop_no in enumerate(message.shape)
+            )
+        )
+        piece_out = jnp.zeros(t_next, message.dtype)
+        x_new = lax.dynamic_update_slice_in_dim(
+            piece_out, message, q_next * current_value, axis=on_dim
+        )
+        v1 = vec_out = message
+        for d in range(1, formed // 2 + 1):
+            block_out = tuple(((dev, (dev + 1) % formed) for dev in range(formed)))
+            v1 = lax.ppermute(v1, peer_axis, block_out)
+            x_new = lax.dynamic_update_slice_in_dim(
+                x_new, v1, (q_next - d) % formed * current_value, axis=on_dim
+            )
+            if 2 * d < formed:
+                local_out = tuple(((dev, (dev - 1) % formed) for dev in range(formed)))
+                vec_out = lax.ppermute(vec_out, peer_axis, local_out)
+                x_new = lax.dynamic_update_slice_in_dim(
+                    x_new, vec_out, (q_next + d) % formed * current_value, axis=on_dim
+                )
+        return x_new
+
     return (
-        lax.all_gather(local_pair[0], "fsdp", axis=1, tiled=True),
+        process_terms(1, "fsdp", local_pair[0]),
         lax.all_gather(local_pair[1], "fsdp", axis=1, tiled=True),
     )
 

time: 1010 us -> 1090 us (1.079)
  starting transfers between devices: 18.3 us -> 100 us
  waiting for transfers between devices: 477 us -> 422 us
  local copies, waits for them, and re-layouts: 66.9 us -> 107 us
  blocking collectives: 126 us -> 146 us
    all_gather x1 -> x0, waiting for transfers between devices: 87.4 us -> none  [gather_experts(): lax.all_gather(local_pair[0], 'fsdp', axis=1, tiled=True)]
    ppermute x0 -> x15, starting transfers between devices: none -> 82.4 us  [the longest x8 71.8 us: process_terms(): v1 = lax.ppermute(v1, peer_axis, block_out)]
    ppermute x0 -> x15, waiting for transfers between devices: none -> 55.9 us  [the longest x8 55.9 us: process_terms(): v1 = lax.ppermute(v1, peer_axis, block_out)]
    dynamic_update_slice x0 -> x16, local copies, waits for them, and re-layouts: none -> 34.7 us  [the longest x8 18 us: process_terms(): lax.dynamic_update_slice_in_dim(x_new, v1, (q_next - d) % formed * curren...]
    unnamed x2, blocking collectives: 85.2 us -> 105 us
  transfers between devices with their start and end apart: 12 -> 26, of which waited for: 9 -> 10; matrix products, arithmetic and copies ran while one was open for 31% -> 31% of each run, Pallas kernels for 0% -> 0%
where the time goes in v1:
time: 1090 us
  waiting for transfers between devices  422 us (39%)
  matrix products  274 us (25%)
  blocking collectives  146 us (13%)
  local copies, waits for them, and re-layouts  107 us (10%)
  starting transfers between devices  100 us (9%)
  other arithmetic  22.5 us (2%)
  between operations  15.2 us (1%)
    reduce_scatter x1, waiting for transfers between devices, per_device(): lax.psum_scatter(d_qkv, ('dp', 'fsdp'), scatter_dimension=0, tiled=True)  125 us
    unnamed x2, blocking collectives  105 us
    reduce_scatter x1, waiting for transfers between devices, per_device(): lax.psum_scatter(d_proj, ('dp', 'fsdp'), scatter_dimension=0, tiled=True)  102 us
    reduce_scatter x1, waiting for transfers between devices, reduce_experts(): lax.psum_scatter(grad_down.astype(jnp.bfloat16), 'fsdp', scatter_dimensio...  88.8 us
    ppermute x8, starting transfers between devices, process_terms(): v1 = lax.ppermute(v1, peer_axis, block_out)  71.8 us
    ppermute x8, waiting for transfers between devices, process_terms(): v1 = lax.ppermute(v1, peer_axis, block_out)  55.9 us
    all_gather x1, blocking collectives, gather_dense(): lax.all_gather(w_router, ('dp', 'fsdp'), axis=0, tiled=True)  41.3 us
    dot_general x1, matrix products, expert_forward(): jnp.einsum('ecd,edf->ecf', expert_rows, w_up, preferred_element_type=jnp....  26.7 us
  transfers between devices with their start and end apart: 26, of which 10 were waited for; matrix products, arithmetic and copies ran while one was open for 31% of the time, Pallas kernels for 0%

profile of v1, /device:TPU:0, one launch (start us, length us, event | category | flops | bytes accessed | tf_op | source)
XLA Modules:
  0.0 1087.1 jit_solution(9432802819747360128)
XLA Ops:
  10.0 5.0 collective-permute-start.1
  15.0 14.8 %collective-permute-done = bf16[4,48,3072]{2,1,0:T(8,128)(2,1)S(1)} collective-permute-done((bf16[4,48,3072]{2,1,0:T(8,128)(2,1)}, bf16[4,48,3072]{2,1,0:T(8,128)(2,1)S(1)}, u32[]{:S(2)}, u32[]{:S(2)}) %collective-permute-start) | collective-permute-done | bytes 1179680 | tf_op jit(solution)/shard_map/ppermute | solution.py:124
  29.9 9.6 collective-permute-start.2
  39.7 9.8 collective-permute-done.2
  49.5 19.3 %collective-permute-start.4 = (bf16[4,48,3072]{2,1,0:T(8,128)(2,1)}, bf16[4,48,3072]{2,1,0:T(8,128)(2,1)}, u32[]{:S(2)}, u32[]{:S(2)}) collective-permute-start(bf16[4,48,3072]{2,1,0:T(8,128)(2,1)} %collective-permute-done.2), channel_id=1, source_target_pairs={{0,1},{1,2},{2,3},{3,4},{4,5},{5,6},{6,7},{7,8},{8,9},{9,10},{10,1... | collective-permute-start | bytes 3538952 | tf_op jit(solution)/shard_map/ppermute | solution.py:124
  69.9 6.8 broadcast.138
  77.8 24.9 %collective-permute-start.6 = (bf16[4,48,3072]{2,1,0:T(8,128)(2,1)}, bf16[4,48,3072]{2,1,0:T(8,128)(2,1)}, u32[]{:S(2)}, u32[]{:S(2)}) collective-permute-start(bf16[4,48,3072]{2,1,0:T(8,128)(2,1)} %collective-permute-done.4), channel_id=1, source_target_pairs={{0,1},{1,2},{2,3},{3,4},{4,5},{5,6},{6,7},{7,8},{8,9},{9,10},{10,1... | collective-permute-start | bytes 3538952 | tf_op jit(solution)/shard_map/ppermute | solution.py:124
  103.8 63.7 %all-reduce.6 = (bf16[768]{0:T(1024)(128)(2,1)S(1)}, bf16[768]{0:T(1024)(128)(2,1)S(1)}) all-reduce(bf16[768]{0:T(1024)(128)(2,1)S(1)} %dynamic-update-slice, bf16[768]{0:T(1024)(128)(2,1)S(1)} %dynamic-update-slice.1), channel_id=1, replica_groups=mesh['dp'=2,'fsdp'=16] {'dp','fsdp'}, use_global_device_ids=true, to_apply=%add | all-reduce | flops 1536 | bytes 6144
  167.5 41.3 %all-gather = bf16[32,24,8]{1,2,0:T(8,128)(2,1)S(1)} all-gather(bf16[1,24,8]{1,2,0:T(8,128)(2,1)S(1)} %bitcast.199), channel_id=1, replica_groups=mesh['dp'=2,'fsdp'=16] {'dp','fsdp'}, dimensions={0}, use_global_device_ids=true | all-gather | bytes 12672 | tf_op jit(solution)/shard_map/all_gather | solution.py:100
  229.0 31.3 %collective-permute-done.8 = bf16[4,48,3072]{2,1,0:T(8,128)(2,1)} collective-permute-done((bf16[4,48,3072]{2,1,0:T(8,128)(2,1)}, bf16[4,48,3072]{2,1,0:T(8,128)(2,1)}, u32[]{:S(2)}, u32[]{:S(2)}) %collective-permute-start.8) | collective-permute-done | bytes 1179680 | tf_op jit(solution)/shard_map/ppermute | solution.py:124
  260.3 11.2 %collective-permute-start.10 = (bf16[4,48,3072]{2,1,0:T(8,128)(2,1)}, bf16[4,48,3072]{2,1,0:T(8,128)(2,1)}, u32[]{:S(2)}, u32[]{:S(2)}) collective-permute-start(bf16[4,48,3072]{2,1,0:T(8,128)(2,1)} %collective-permute-done.8), channel_id=1, source_target_pairs={{0,1},{1,2},{2,3},{3,4},{4,5},{5,6},{6,7},{7,8},{8,9},{9,10},{10,1... | collective-permute-start | bytes 3538952 | tf_op jit(solution)/shard_map/ppermute | solution.py:124
  271.7 5.9 convolution_convert_fusion.3
  289.8 37.7 %while.26 = (s32[]{:T(128)}, bf16[12,1,576,64]{2,3,1,0:T(8,128)(2,1)}, f32[12,1,576]{2,1,0:T(1,128)}, bf16[12,1,576,64]{3,2,1,0:T(8,128)(2,1)S(1)}, bf16[12,1,57...) while((s32[]{:T(128)}, bf16[12,1,576,64]{2,3,1,0:T(8,128)(2,1)}, ...), condition=%wide.region_5.6_spmd, body=%wide.region_2.5_spmd.sunk | while | flops 87293376 | bytes 4531033 | solution.py:167
  356.0 9.0 all-to-all-done.2
  381.2 12.4 %all-to-all-done = bf16[8,152,768]{2,1,0:T(8,128)(2,1)} async-done(((bf16[8,152,768]{2,1,0:T(8,128)(2,1)}), bf16[8,152,768]{2,1,0:T(8,128)(2,1)}, u32[]{:S(2)}, u32[]{:S(2)}) %all-to-all-start) | async-done | bytes 1867808 | tf_op jit(solution)/shard_map/all_to_all | solution.py:193
  402.4 12.9 %fusion.77 = f32[4,304,3072]{2,1,0:T(8,128)} fusion(bf16[4,304,768]{2,1,0:T(8,128)(2,1)S(1)} %bitcast.182, bf16[4,3072,768]{2,1,0:T(8,128)(2,1)} %all-gather.9.cloned.1.call-done), kind=kOutput, calls=%fused_computation.157 | convolution fusion | flops 5737807872 | bytes 35684352 | tf_op jit(solution)/shard_map/ecd,efd->ecf/dot_general | solution.py:81
  415.3 26.7 %fusion.43 = (bf16[4,304,3072]{2,1,0:T(8,128)(2,1)}, f32[4,304,3072]{2,1,0:T(8,128)}) fusion(f32[4,304,3072]{2,1,0:T(8,128)} %fusion.77, bf16[4,304,768]{2,1,0:T(8,128)(2,1)} %bitcast.192, bf16[4,768,3072]{2,1,0:T(8,128)(2,1)} %constant_dynamic-update-slice_fusion), kind=kOutput, calls=%fused_computation.59 | convolution fusion | flops 5812518912 | bytes 58097664 | tf_op jit(solution)/shard_map/ecd,edf->ecf/dot_general | solution.py:72
  442.0 16.5 %convolution_convert_fusion.2 = bf16[4,768,3072]{2,1,0:T(8,128)(2,1)} fusion(bf16[4,304,768]{2,1,0:T(8,128)(2,1)} %bitcast.193, bf16[4,304,3072]{2,1,0:T(8,128)(2,1)} %get-tuple-element.212), kind=kOutput, calls=%fused_computation.62 | convolution fusion | flops 5747245056 | bytes 28213248 | tf_op jit(solution)/shard_map/ecd,ecf->edf/dot_general | solution.py:87
  458.7 20.0 %convolution_convert_fusion.1 = bf16[4,3072,768]{2,1,0:T(8,128)(2,1)} fusion(bf16[4,304,768]{2,1,0:T(8,128)(2,1)S(1)} %bitcast.183, f32[4,304,3072]{2,1,0:T(8,128)} %get-tuple-element.213), kind=kOutput, calls=%fused_computation.61 | convolution fusion | flops 5780865024 | bytes 35684352 | tf_op jit(solution)/shard_map/ecf,ecd->efd/dot_general | solution.py:86
  478.8 19.1 %convolution_convert_fusion.7 = bf16[4,304,768]{2,1,0:T(8,128)(2,1)S(1)} fusion(bf16[4,3072,768]{2,1,0:T(8,128)(2,1)} %all-gather.9.cloned.1.call-done, f32[4,304,3072]{2,1,0:T(8,128)} %get-tuple-element.213), kind=kOutput, calls=%fused_computation.85 | convolution fusion | flops 5772361728 | bytes 35684352 | tf_op jit(solution)/shard_map/ecf,efd->ecd/dot_general | solution.py:74
  504.0 13.2 %convolution_convert_fusion.6 = bf16[4,304,768]{2,1,0:T(8,128)(2,1)} fusion(bf16[4,304,3072]{2,1,0:T(8,128)(2,1)} %get-tuple-element.212, bf16[4,768,3072]{2,1,0:T(8,128)(2,1)} %constant_dynamic-update-slice_fusion), kind=kOutput, calls=%fused_computation.84 | convolution fusion | flops 5738741760 | bytes 28213248 | tf_op jit(solution)/shard_map/ecf,edf->ecd/dot_general | solution.py:88
  521.0 6.6 all-to-all-done.1
  535.8 20.7 %all-to-all-done.3 = bf16[4,304,768]{2,0,1:T(4,128)(2,1)} async-done(((bf16[4,304,768]{2,0,1:T(4,128)(2,1)}), bf16[4,304,768]{2,0,1:T(4,128)(2,1)}, u32[]{:S(2)}, u32[]{:S(2)}) %all-to-all-start.3) | async-done | bytes 1867808 | tf_op jit(solution)/shard_map/all_to_all | solution.py:224
  559.6 4.8 gather_fusion
  569.1 6.0 fusion.62
  590.6 100.8 %while.27 = (s32[]{:T(128)}, bf16[12,1,576,64]{2,3,1,0:T(8,128)(2,1)}, bf16[12,1,576,64]{2,3,1,0:T(8,128)(2,1)}, bf16[12,1,576,64]{2,3,1,0:T(8,128)(2,1)}, bf16[...) while((s32[]{:T(128)}, ...), condition=%wide.region_19.20_spmd, body=%wide.region_17.19_spmd.sunk | while | flops 215064000 | bytes 11510129 | solution.py:238
  695.3 5.5 fusion.71
  702.2 7.2 fusion.60
  709.3 41.1 %all-reduce.5 = (f32[768]{0:T(1024)S(1)}, f32[768]{0:T(1024)S(1)}, f32[768,8]{0,1:T(8,128)S(1)}) all-reduce(f32[768]{0:T(1024)S(1)} %get-tuple-element.158, f32[768]{0:T(1024)S(1)} %get-tuple-element.156, f32[768,8]{0,1:T(8,128)S(1)} %fusion.79), channel_id=2, replica_groups=mesh['dp'=2,'fsdp'=16] {'dp','fsdp'}, use_global_device_ids=true, to_apply=%region_23.24.clone | all-reduce | flops 7680 | bytes 61440
  761.6 88.8 %reduce-scatter.12.cloned.1.call-done = bf16[4,192,768]{2,1,0:T(8,128)(2,1)} async-done(((bf16[4,3072,768]{2,1,0:T(8,128)(2,1)}), bf16[4,192,768]{2,1,0:T(8,128)(2,1)}) %reduce-scatter.12.cloned.1.call-update) | async-done | bytes 1179664 | tf_op jit(solution)/shard_map/reduce_scatter | solution.py:147
  853.2 101.7 %reduce-scatter.8.cloned.1.call-done = f32[24,768]{1,0:T(8,128)} async-done(((f32[768,768]{1,0:T(8,128)}), f32[24,768]{1,0:T(8,128)}) %reduce-scatter.8.cloned.1.call-update) | async-done | bytes 73744 | tf_op jit(solution)/shard_map/reduce_scatter | solution.py:256
  954.9 124.9 %reduce-scatter.6.cloned.1.call-done = f32[24,2304]{1,0:T(8,128)} async-done(((f32[768,2304]{1,0:T(8,128)}), f32[24,2304]{1,0:T(8,128)}) %reduce-scatter.6.cloned.1.call-update) | async-done | bytes 221200 | tf_op jit(solution)/shard_map/reduce_scatter | solution.py:255
  (362 shorter events, 290.8 us)
Async XLA Ops:
  7.2 62.0 %copy-start.26 = (s32[576,2]{0,1:T(2,128)S(1)}, s32[576,2]{0,1:T(2,128)}, u32[]{:S(2)}) copy-start(s32[576,2]{0,1:T(2,128)} %param.24) | copy-start | bytes 13828
  7.2 62.0 %copy-start.28 = (s32[576,2]{0,1:T(2,128)S(1)}, s32[576,2]{0,1:T(2,128)}, u32[]{:S(2)}) copy-start(s32[576,2]{0,1:T(2,128)} %param.23) | copy-start | bytes 13828
  7.2 264.5 %all-gather.5.cloned.1.call-start = ((), (), s32[]{:S(2)}) async-start(), calls=%async_computation.8 | async-start | bytes 3649536 | tf_op jit(solution)/shard_map/all_gather | solution.py:97
  7.9 319.6 %all-gather.7.cloned.1.call-start = ((), (), s32[]{:S(2)}) async-start(), calls=%async_computation.9 | async-start | bytes 1216512 | tf_op jit(solution)/shard_map/all_gather | solution.py:98
  8.7 393.7 %all-gather.9.cloned.1.call-start = ((), (), s32[]{:S(2)}) async-start(), calls=%async_computation.10 | async-start | bytes 20054016 | tf_op jit(solution)/shard_map/all_gather | solution.py:138
  9.4 20.4 %collective-permute-start = (bf16[4,48,3072]{2,1,0:T(8,128)(2,1)}, bf16[4,48,3072]{2,1,0:T(8,128)(2,1)S(1)}, u32[]{:S(2)}, u32[]{:S(2)}) collective-permute-start(bf16[4,48,3072]{2,1,0:T(8,128)(2,1)} %param.21), channel_id=1, source_target_pairs={{0,1},{1,2},{2,3},{3,4},{4,5},{5,6},{6,7},{7,8},{8,9},{9,10},{10,1... | collective-permute-start | bytes 3538952 | tf_op jit(solution)/shard_map/ppermute | solution.py:124
  10.0 29.5 %collective-permute-start.1 = (bf16[4,48,3072]{2,1,0:T(8,128)(2,1)}, bf16[4,48,3072]{2,1,0:T(8,128)(2,1)}, u32[]{:S(2)}, u32[]{:S(2)}) collective-permute-start(bf16[4,48,3072]{2,1,0:T(8,128)(2,1)} %param.21), channel_id=1, source_target_pairs={{0,15},{1,0},{2,1},{3,2},{4,3},{5,4},{6,5},{7,6},{8,7},{9,8},{10,9... | collective-permute-start | bytes 3538952 | tf_op jit(solution)/shard_map/ppermute | solution.py:130
  29.9 19.6 %collective-permute-start.2 = (bf16[4,48,3072]{2,1,0:T(8,128)(2,1)S(1)}, bf16[4,48,3072]{2,1,0:T(8,128)(2,1)}, u32[]{:S(2)}, u32[]{:S(2)}) collective-permute-start(bf16[4,48,3072]{2,1,0:T(8,128)(2,1)S(1)} %collective-permute-done), channel_id=1, source_target_pairs={{0,1},{1,2},{2,3},{3,4},{4,5},{5,6},{6,7},{7,8},{8,9},{9,10},{10,1... | collective-permute-start | bytes 3538952 | tf_op jit(solution)/shard_map/ppermute | solution.py:124
  39.5 29.3 %collective-permute-start.3 = (bf16[4,48,3072]{2,1,0:T(8,128)(2,1)}, bf16[4,48,3072]{2,1,0:T(8,128)(2,1)S(1)}, u32[]{:S(2)}, u32[]{:S(2)}) collective-permute-start(bf16[4,48,3072]{2,1,0:T(8,128)(2,1)} %collective-permute-done.1), channel_id=1, source_target_pairs={{0,15},{1,0},{2,1},{3,2},{4,3},{5,4},{6,5},{7,6},{8,7},{9,8},{10,9... | collective-permute-start | bytes 3538952 | tf_op jit(solution)/shard_map/ppermute | solution.py:130
  49.5 28.4 %collective-permute-start.4 = (bf16[4,48,3072]{2,1,0:T(8,128)(2,1)}, bf16[4,48,3072]{2,1,0:T(8,128)(2,1)}, u32[]{:S(2)}, u32[]{:S(2)}) collective-permute-start(bf16[4,48,3072]{2,1,0:T(8,128)(2,1)} %collective-permute-done.2), channel_id=1, source_target_pairs={{0,1},{1,2},{2,3},{3,4},{4,5},{5,6},{6,7},{7,8},{8,9},{9,10},{10,1... | collective-permute-start | bytes 3538952 | tf_op jit(solution)/shard_map/ppermute | solution.py:124
  68.8 33.9 %collective-permute-start.5 = (bf16[4,48,3072]{2,1,0:T(8,128)(2,1)S(1)}, bf16[4,48,3072]{2,1,0:T(8,128)(2,1)}, u32[]{:S(2)}, u32[]{:S(2)}) collective-permute-start(bf16[4,48,3072]{2,1,0:T(8,128)(2,1)S(1)} %collective-permute-done.3), channel_id=1, source_target_pairs={{0,15},{1,0},{2,1},{3,2},{4,3},{5,4},{6,5},{7,6},{8,7},{9,8},{10,9... | collective-permute-start | bytes 3538952 | tf_op jit(solution)/shard_map/ppermute | solution.py:130
  68.8 202.9 %copy-start.30 = (f32[576]{0:T(1024)}, f32[576]{0:T(1024)S(1)}, u32[]{:S(2)}) copy-start(f32[576]{0:T(1024)S(1)} %broadcast_multiply_fusion.5) | copy-start | bytes 6916
  69.2 202.5 %copy-start.34 = (f32[576]{0:T(1024)}, f32[576]{0:T(1024)S(1)}, u32[]{:S(2)}) copy-start(f32[576]{0:T(1024)S(1)} %add_rsqrt_fusion.1) | copy-start | bytes 6916
  76.7 90.8 %copy-start.39 = (bf16[24,8]{0,1:T(8,128)(2,1)S(1)}, bf16[24,8]{0,1:T(8,128)(2,1)}, u32[]{:S(2)}) copy-start(bf16[24,8]{0,1:T(8,128)(2,1)} %param.20) | copy-start | bytes 1156
  77.8 138.4 %collective-permute-start.6 = (bf16[4,48,3072]{2,1,0:T(8,128)(2,1)}, bf16[4,48,3072]{2,1,0:T(8,128)(2,1)}, u32[]{:S(2)}, u32[]{:S(2)}) collective-permute-start(bf16[4,48,3072]{2,1,0:T(8,128)(2,1)} %collective-permute-done.4), channel_id=1, source_target_pairs={{0,1},{1,2},{2,3},{3,4},{4,5},{5,6},{6,7},{7,8},{8,9},{9,10},{10,1... | collective-permute-start | bytes 3538952 | tf_op jit(solution)/shard_map/ppermute | solution.py:124
  102.7 113.9 %collective-permute-start.7 = (bf16[4,48,3072]{2,1,0:T(8,128)(2,1)}, bf16[4,48,3072]{2,1,0:T(8,128)(2,1)S(1)}, u32[]{:S(2)}, u32[]{:S(2)}) collective-permute-start(bf16[4,48,3072]{2,1,0:T(8,128)(2,1)} %collective-permute-done.5), channel_id=1, source_target_pairs={{0,15},{1,0},{2,1},{3,2},{4,3},{5,4},{6,5},{7,6},{8,7},{9,8},{10,9... | collective-permute-start | bytes 3538952 | tf_op jit(solution)/shard_map/ppermute | solution.py:130
  167.5 104.2 %copy-start.36 = (f32[768]{0:T(1024)}, f32[768]{0:T(1024)S(1)}, u32[]{:S(2)}) copy-start(f32[768]{0:T(1024)S(1)} %convert_element_type.101) | copy-start | bytes 9220
  216.2 44.0 %collective-permute-start.8 = (bf16[4,48,3072]{2,1,0:T(8,128)(2,1)}, bf16[4,48,3072]{2,1,0:T(8,128)(2,1)}, u32[]{:S(2)}, u32[]{:S(2)}) collective-permute-start(bf16[4,48,3072]{2,1,0:T(8,128)(2,1)} %collective-permute-done.6), channel_id=1, source_target_pairs={{0,1},{1,2},{2,3},{3,4},{4,5},{5,6},{6,7},{7,8},{8,9},{9,10},{10,1... | collective-permute-start | bytes 3538952 | tf_op jit(solution)/shard_map/ppermute | solution.py:124
  216.6 54.8 %collective-permute-start.9 = (bf16[4,48,3072]{2,1,0:T(8,128)(2,1)S(1)}, bf16[4,48,3072]{2,1,0:T(8,128)(2,1)}, u32[]{:S(2)}, u32[]{:S(2)}) collective-permute-start(bf16[4,48,3072]{2,1,0:T(8,128)(2,1)S(1)} %collective-permute-done.7), channel_id=1, source_target_pairs={{0,15},{1,0},{2,1},{3,2},{4,3},{5,4},{6,5},{7,6},{8,7},{9,8},{10,9... | collective-permute-start | bytes 3538952 | tf_op jit(solution)/shard_map/ppermute | solution.py:130
  260.3 83.5 %collective-permute-start.10 = (bf16[4,48,3072]{2,1,0:T(8,128)(2,1)}, bf16[4,48,3072]{2,1,0:T(8,128)(2,1)}, u32[]{:S(2)}, u32[]{:S(2)}) collective-permute-start(bf16[4,48,3072]{2,1,0:T(8,128)(2,1)} %collective-permute-done.8), channel_id=1, source_target_pairs={{0,1},{1,2},{2,3},{3,4},{4,5},{5,6},{6,7},{7,8},{8,9},{9,10},{10,1... | collective-permute-start | bytes 3538952 | tf_op jit(solution)/shard_map/ppermute | solution.py:124
  271.5 83.2 %collective-permute-start.11 = (bf16[4,48,3072]{2,1,0:T(8,128)(2,1)}, bf16[4,48,3072]{2,1,0:T(8,128)(2,1)}, u32[]{:S(2)}, u32[]{:S(2)}) collective-permute-start(bf16[4,48,3072]{2,1,0:T(8,128)(2,1)} %collective-permute-done.9), channel_id=1, source_target_pairs={{0,15},{1,0},{2,1},{3,2},{4,3},{5,4},{6,5},{7,6},{8,7},{9,8},{10,9... | collective-permute-start | bytes 3538952 | tf_op jit(solution)/shard_map/ppermute | solution.py:130
  340.0 25.0 %all-to-all-start.2 = ((bf16[8,152,768]{2,1,0:T(8,128)(2,1)}), bf16[8,152,768]{2,1,0:T(8,128)(2,1)S(1)}, u32[]{:S(2)}, u32[]{:S(2)}) async-start(bf16[8,152,768]{2,1,0:T(8,128)(2,1)} %bitcast.191), calls=%async_computation.2 | async-start | bytes 3735552 | tf_op jit(solution)/shard_map/all_to_all | solution.py:220
  343.7 29.8 %collective-permute-start.12 = (bf16[4,48,3072]{2,1,0:T(8,128)(2,1)}, bf16[4,48,3072]{2,1,0:T(8,128)(2,1)}, u32[]{:S(2)}, u32[]{:S(2)}) collective-permute-start(bf16[4,48,3072]{2,1,0:T(8,128)(2,1)} %collective-permute-done.10), channel_id=1, source_target_pairs={{0,1},{1,2},{2,3},{3,4},{4,5},{5,6},{6,7},{7,8},{8,9},{9,10},{10,1... | collective-permute-start | bytes 3538952 | tf_op jit(solution)/shard_map/ppermute | solution.py:124
  354.6 44.2 %collective-permute-start.13 = (bf16[4,48,3072]{2,1,0:T(8,128)(2,1)}, bf16[4,48,3072]{2,1,0:T(8,128)(2,1)}, u32[]{:S(2)}, u32[]{:S(2)}) collective-permute-start(bf16[4,48,3072]{2,1,0:T(8,128)(2,1)} %collective-permute-done.11), channel_id=1, source_target_pairs={{0,15},{1,0},{2,1},{3,2},{4,3},{5,4},{6,5},{7,6},{8,7},{9,8},{10,9... | collective-permute-start | bytes 3538952 | tf_op jit(solution)/shard_map/ppermute | solution.py:130
  366.2 27.4 %all-to-all-start = ((bf16[8,152,768]{2,1,0:T(8,128)(2,1)}), bf16[8,152,768]{2,1,0:T(8,128)(2,1)}, u32[]{:S(2)}, u32[]{:S(2)}) async-start(bf16[8,152,768]{2,1,0:T(8,128)(2,1)} %bitcast.190), calls=%async_computation | async-start | bytes 3735552 | tf_op jit(solution)/shard_map/all_to_all | solution.py:193
  371.1 387.6 %reduce-scatter.10.cloned.1.call-start = ((), (), s32[]{:S(2)}) async-start(), calls=%async_computation.13 | async-start | bytes 20054016 | tf_op jit(solution)/shard_map/reduce_scatter | solution.py:144
  373.5 27.8 %collective-permute-start.14 = (bf16[4,48,3072]{2,1,0:T(8,128)(2,1)}, bf16[4,48,3072]{2,1,0:T(8,128)(2,1)S(1)}, u32[]{:S(2)}, u32[]{:S(2)}) collective-permute-start(bf16[4,48,3072]{2,1,0:T(8,128)(2,1)} %collective-permute-done.12), channel_id=1, source_target_pairs={{0,1},{1,2},{2,3},{3,4},{4,5},{5,6},{6,7},{7,8},{8,9},{9,10},{10,1... | collective-permute-start | bytes 3538952 | tf_op jit(solution)/shard_map/ppermute | solution.py:124
  458.5 391.9 %reduce-scatter.12.cloned.1.call-start = ((), (), s32[]{:S(2)}) async-start(), calls=%async_computation.14 | async-start | bytes 20054016 | tf_op jit(solution)/shard_map/reduce_scatter | solution.py:147
  500.1 27.5 %all-to-all-start.1 = ((bf16[4,304,768]{2,0,1:T(4,128)(2,1)}), bf16[4,304,768]{2,0,1:T(4,128)(2,1)S(1)}, u32[]{:S(2)}, u32[]{:S(2)}) async-start(bf16[4,304,768]{2,0,1:T(4,128)(2,1)} %copy.108), calls=%async_computation.1 | async-start | bytes 3735552 | tf_op jit(solution)/shard_map/all_to_all | solution.py:195
  528.9 27.7 %all-to-all-start.3 = ((bf16[4,304,768]{2,0,1:T(4,128)(2,1)}), bf16[4,304,768]{2,0,1:T(4,128)(2,1)}, u32[]{:S(2)}, u32[]{:S(2)}) async-start(bf16[4,304,768]{2,0,1:T(4,128)(2,1)} %copy.112), calls=%async_computation.3 | async-start | bytes 3735552 | tf_op jit(solution)/shard_map/all_to_all | solution.py:224
  533.6 421.3 %reduce-scatter.8.cloned.1.call-start = ((), (), s32[]{:S(2)}) async-start(), calls=%async_computation.12 | async-start | bytes 2433024 | tf_op jit(solution)/shard_map/reduce_scatter | solution.py:256
  590.3 489.5 %reduce-scatter.6.cloned.1.call-start = ((), (), s32[]{:S(2)}) async-start(), calls=%async_computation.11 | async-start | bytes 7299072 | tf_op jit(solution)/shard_map/reduce_scatter | solution.py:255
  (37 other events, 301.3 us)
Sparse Core Ops, SparseCore 0:
  10.9 86.0 all-gather.4
  100.0 60.7 all-gather.6
  162.4 141.8 all-gather.8
  458.6 193.5 reduce-scatter.9
  656.2 194.1 reduce-scatter.11
  856.1 98.7 reduce-scatter.7
  961.2 118.5 reduce-scatter.5
